TPU v7x, 32 devices: a whole 2x2x4 slice. The times are simulated.
32 devices in a mesh: gy: 4 (over x, core), gz: 2 (over y), ga: 4 (over z).
Axes of the slice: x: 2, y: 2, z: 4, core: 2. Of those that a mesh axis runs over, the one named last changes fastest.
Arguments:
- fields: float32 [16, 256, 8, 512], P(None, 'gy', 'gz', 'ga'), may hold values from -6 to 6
- section_start: float32 [16, 256, 8, 512], P(None, 'gy', 'gz', 'ga'), may hold values from -6 to 6
- velocity: float32 [3, 256, 8, 512], P(None, 'gy', 'gz', 'ga'), may hold values from -4 to 4
- diffusivity: float32 [16], replicated, may hold values from 0.02 to 0.2
- reaction: float32 [16, 16], replicated, may hold values from -1.5 to 1.5
- x_factor: bfloat16 [512, 64], replicated, may hold values from -0.25 to 0.25
- y_factor: float32 [256, 64], replicated, may hold values from -6 to 6
Outputs:
- new_fields: float32 [16, 256, 8, 512], P(None, 'gy', 'gz', 'ga')
- x_gram: float32 [512, 512], P(('gy', 'gz'))
- y_products: float32 [8, 256, 64], P(('gz', 'gy'))
All inputs are finite; a program needn't handle non-finite values.
Results may differ from a plain program's by a relative error of at most 0.0028.
Values may be sent and summed in bfloat16 or wider, within the bound.
No kernel may reach another device: no remote copies, remote signals or barrier semaphores. Data moves between devices by JAX's collectives and lax.ppermute only.
A program may use at most 64 MiB of HBM per device.

v0:
```python
import jax
import jax.numpy as jnp
from jax import lax
from jax.sharding import PartitionSpec as P

time_step = 0.4


def with_halo(block, sides, width):
    for axis, dim in sides:
        count = lax.axis_size(axis)
        forward = [(i, i + 1) for i in range(count - 1)]
        backward = [(target, source) for source, target in forward]
        low = lax.ppermute(
            lax.slice_in_dim(block, block.shape[dim] - width, None, axis=dim), axis, forward
        )
        high = lax.ppermute(lax.slice_in_dim(block, 0, width, axis=dim), axis, backward)
        block = jnp.concatenate([low, block, high], axis=dim)
    return block


def shards(fields, section_start, velocity, diffusivity, reaction, x_factor, y_factor):
    padded = with_halo(fields, (("gy", 1), ("gz", 2), ("ga", 3)), 1)
    center = padded[:, 1:-1, 1:-1, 1:-1]
    y_plus = padded[:, 2:, 1:-1, 1:-1]
    y_minus = padded[:, :-2, 1:-1, 1:-1]
    z_plus = padded[:, 1:-1, 2:, 1:-1]
    z_minus = padded[:, 1:-1, :-2, 1:-1]
    x_plus = padded[:, 1:-1, 1:-1, 2:]
    x_minus = padded[:, 1:-1, 1:-1, :-2]
    laplace_sum = y_plus + y_minus + z_plus + z_minus + x_plus + x_minus - 6.0 * center
    advection = (
        velocity[0][None] * (x_plus - x_minus) * 0.5
        + velocity[1][None] * (y_plus - y_minus) * 0.5
        + velocity[2][None] * (z_plus - z_minus) * 0.5
    )
    diffusion = diffusivity[:, None, None, None]
    tendency = (
        diffusion * laplace_sum
        - advection
        + jnp.einsum("vw,wyzx->vyzx", reaction, fields, precision=lax.Precision.HIGHEST)
    )
    section_value = 0.75 * section_start + 0.25 * (fields + time_step * tendency)
    buffer_rank = lax.axis_index("ga") == lax.axis_size("ga") - 1
    new_fields = jnp.where(buffer_rank, fields, section_value)
    snapshot = new_fields.astype(jnp.bfloat16)
    devices = lax.axis_size("gy") * lax.axis_size("gz")
    rank_x = x_factor.shape[1]
    gathered = lax.all_gather(snapshot, "ga", axis=3, tiled=True)
    variables, y_cells, z_cells, x_cells = gathered.shape
    unfolded = gathered.reshape(variables * y_cells * z_cells, x_cells)
    cell_count = float(variables * y_cells * z_cells * devices)
    gram_rows = lax.psum_scatter(
        lax.dot_general(
            unfolded, unfolded, (((0,), (0,)), ((), ())), preferred_element_type=jnp.float32
        ),
        ("gy", "gz"),
        scatter_dimension=0,
        tiled=True,
    )
    x_gram = gram_rows / cell_count
    projected = jnp.einsum(
        "vyzx,xr->yzvr", gathered, x_factor, preferred_element_type=jnp.float32
    ).astype(jnp.bfloat16)
    projected = projected.reshape(y_cells, z_cells, variables * rank_x)
    full_y = lax.all_to_all(projected, "gy", split_axis=1, concat_axis=0, tiled=True)
    y_gram = jnp.einsum("yzc,wzc->zyw", full_y, full_y, preferred_element_type=jnp.float32) / float(
        variables * rank_x
    )
    y_products = jnp.einsum("zyw,wk->zyk", y_gram, y_factor, precision=lax.Precision.HIGHEST)
    return (new_fields, x_gram, y_products)


def solution(mesh):
    in_specs = (
        P(None, "gy", "gz", "ga"),
        P(None, "gy", "gz", "ga"),
        P(None, "gy", "gz", "ga"),
        P(),
        P(),
        P(),
        P(),
    )
    out_specs = (P(None, "gy", "gz", "ga"), P(("gy", "gz"), None), P(("gz", "gy"), None, None))
    return jax.shard_map(shards, mesh=mesh, in_specs=in_specs, out_specs=out_specs, check_vma=False)
```

profile of v0, /device:TPU:0, one launch (start us, length us, event | category | flops | bytes accessed | tf_op | source)
XLA Modules:
  0.0 199.7 jit_solution(294682262062690017)
XLA Ops:
  7.2 3.0 %copy.52 = f32[16,64,4,128]{3,0,2,1:T(8,128)S(1)} copy(f32[16,64,4,128]{3,2,1,0:T(4,128)} %param.7) | data formatting | bytes 4194304 | tf_op args[0]
  10.2 2.4 %collective-permute-start.1 = (f32[16,1,4,128]{3,0,2,1:T(8,128)S(1)}, f32[16,1,4,128]{3,0,2,1:T(8,128)S(1)}, u32[]{:S(2)}, u32[]{:S(2)}) collective-permute-start(f32[16,1,4,128]{3,0,2,1:T(8,128)S(1)} %get-tuple-element.17), channel_id=1, source_target_pairs={{0,8},{8,16},{16,24},{1,9},{9,17},{17,25},{2,10},{10,18},{18,26},{... | collective-permute-start | bytes 98312 | tf_op jit(solution)/shard_map/ppermute | solution.py:14
  12.6 1.3 collective-permute-start
  15.2 2.6 %collective-permute-done = f32[16,1,4,128]{3,0,2,1:T(8,128)S(1)} collective-permute-done((f32[16,1,4,128]{3,0,2,1:T(8,128)S(1)}, f32[16,1,4,128]{3,0,2,1:T(8,128)S(1)}, u32[]{:S(2)}, u32[]{:S(2)}) %collective-permute-start) | collective-permute-done | bytes 32800 | tf_op jit(solution)/shard_map/ppermute | solution.py:17
  19.2 4.6 %collective-permute-start.3 = (f32[16,66,1,128]{3,0,2,1:T(8,128)S(1)}, f32[16,66,1,128]{3,0,2,1:T(8,128)S(1)}, u32[]{:S(2)}, u32[]{:S(2)}) collective-permute-start(f32[16,66,1,128]{3,0,2,1:T(8,128)S(1)} %get-tuple-element.14), channel_id=1, source_target_pairs={{0,4},{1,5},{2,6},{3,7},{8,12},{9,13},{10,14},{11,15},{16,20},{17,... | collective-permute-start | bytes 1622024 | tf_op jit(solution)/shard_map/ppermute | solution.py:14
  23.8 9.5 %collective-permute-done.2 = f32[16,66,1,128]{3,0,2,1:T(8,128)S(1)} collective-permute-done((f32[16,66,1,128]{3,0,2,1:T(8,128)S(1)}, f32[16,66,1,128]{3,0,2,1:T(8,128)S(1)}, u32[]{:S(2)}, u32[]{:S(2)}) %collective-permute-start.2) | collective-permute-done | bytes 540704 | tf_op jit(solution)/shard_map/ppermute | solution.py:17
  33.3 1.8 collective-permute-done.3
  36.2 2.9 %fusion.12 = (f32[16,66,6,1]{3,0,2,1:T(8,128)}, f32[16,66,6,1]{3,0,2,1:T(8,128)S(1)}) fusion(f32[16,66,6,128]{3,0,2,1:T(8,128)S(1)} %pad_maximum_fusion), kind=kLoop, calls=%fused_computation.30 | loop fusion | bytes 101376 | tf_op jit(solution)/shard_map/slice | solution.py:17
  39.0 2.8 %copy.45 = f32[16,66,6,1]{1,0,3,2:T(8,128)S(1)} copy(f32[16,66,6,1]{3,0,2,1:T(8,128)} %get-tuple-element.12) | data formatting | bytes 50688 | tf_op jit(solution)/shard_map/slice | solution.py:17
  43.1 2.2 %copy.47 = f32[16,66,6,1]{1,0,3,2:T(8,128)} copy(f32[16,66,6,1]{3,0,2,1:T(8,128)S(1)} %get-tuple-element.13) | data formatting | bytes 50688 | tf_op jit(solution)/shard_map/slice | solution.py:15
  45.3 5.2 %collective-permute-start.5 = (f32[16,66,6,1]{1,0,3,2:T(8,128)}, f32[16,66,6,1]{1,0,3,2:T(8,128)}, u32[]{:S(2)}, u32[]{:S(2)}) collective-permute-start(f32[16,66,6,1]{1,0,3,2:T(8,128)} %copy.47), channel_id=1, source_target_pairs={{0,1},{1,2},{2,3},{4,5},{5,6},{6,7},{8,9},{9,10},{10,11},{12,13},{... | collective-permute-start | bytes 76040 | tf_op jit(solution)/shard_map/ppermute | solution.py:14
  50.5 1.8 slice_bitcast_fusion.2
  52.2 2.6 %copy.46 = f32[16,66,6,1]{3,0,2,1:T(8,128)} copy(f32[16,66,6,1]{1,0,3,2:T(8,128)S(1)} %collective-permute-done.4) | data formatting | bytes 50688 | tf_op jit(solution)/shard_map/ppermute | solution.py:17
  54.9 3.6 %copy.48 = f32[16,66,6,1]{3,0,2,1:T(8,128)} copy(f32[16,66,6,1]{1,0,3,2:T(8,128)} %collective-permute-done.5) | data formatting | bytes 50688 | tf_op jit(solution)/shard_map/ppermute | solution.py:14
  58.5 10.6 %fusion.15 = (bf16[16,64,4,128]{3,0,2,1:T(8,128)(2,1)}, f32[16,64,4,128]{3,0,2,1:T(8,128)}) fusion(f32[16,64,4,128]{3,0,2,1:T(8,128)} %copy-done.4, f32[16,16]{1,0:T(8,128)S(1)} %copy-done.14, f32[64,4,128]{2,1,0:T(4,128)} %get-tuple-element.19, f32[64,4,128]{2,1,0:T(4,128)} %get-tuple-element.20, f32[64,4,128]{2,1,0:T(4,128)S(1)} %get-tuple-element.18, ...), kind=kOutput, calls=%fused_computation.33 | convolution fusion | flops 119537664 | bytes 11094593 | tf_op jit(solution)/shard_map/vw,wyzx->vyzx/dot_general | solution.py:41
  69.4 80.7 %all-gather.2.cloned.1.call-done = bf16[16,64,4,512]{3,0,2,1:T(8,128)(2,1)} async-done(((bf16[16,64,4,128]{3,0,2,1:T(8,128)(2,1)}), bf16[16,64,4,512]{3,0,2,1:T(8,128)(2,1)}) %all-gather.2.cloned.1.call-update) | async-done | bytes 4194320 | tf_op jit(solution)/shard_map/all_gather | solution.py:49
  150.1 6.8 %convolution_bitcast_fusion = f32[512,512]{1,0:T(8,128)} fusion(bf16[16,64,4,512]{3,0,2,1:T(8,128)(2,1)} %all-gather.2.cloned.1.call-done), kind=kOutput, calls=%fused_computation.18 | convolution fusion | flops 2147483648 | bytes 5242880 | tf_op jit(solution)/shard_map/dot_general | solution.py:54
  157.0 6.9 %fusion.7 = bf16[64,4,16,64]{3,0,1,2:T(8,128)(2,1)S(1)} fusion(bf16[16,64,4,512]{3,0,2,1:T(8,128)(2,1)} %all-gather.2.cloned.1.call-done, bf16[512,64]{0,1:T(8,128)(2,1)S(1)} %copy-done), kind=kOutput, calls=%fused_computation.17 | convolution fusion | flops 268697600 | bytes 4784128 | tf_op jit(solution)/shard_map/vyzx,xr->yzvr/dot_general | solution.py:62
  164.6 1.5 reshape.22
  166.1 3.5 %all-to-all-start = ((bf16[64,4,1024]{2,0,1:T(8,128)(2,1)}), bf16[64,4,1024]{2,0,1:T(8,128)(2,1)S(1)}, u32[]{:S(2)}, u32[]{:S(2)}) async-start(bf16[64,4,1024]{2,0,1:T(8,128)(2,1)} %reshape.22), calls=%async_computation.1 | async-start | bytes 1048576 | tf_op jit(solution)/shard_map/all_to_all | solution.py:66
  169.6 2.1 %copy.55 = f32[16,64,4,128]{3,2,1,0:T(4,128)} copy(f32[16,64,4,128]{3,0,2,1:T(8,128)S(1)} %copy-done.5) | data formatting | bytes 4194304
  171.7 8.1 %all-to-all-done = bf16[64,4,1024]{2,0,1:T(8,128)(2,1)S(1)} async-done(((bf16[64,4,1024]{2,0,1:T(8,128)(2,1)}), bf16[64,4,1024]{2,0,1:T(8,128)(2,1)S(1)}, u32[]{:S(2)}, u32[]{:S(2)}) %all-to-all-start) | async-done | bytes 524320 | tf_op jit(solution)/shard_map/all_to_all | solution.py:66
  181.2 10.1 %reduce-scatter.2.cloned.1.call-done = f32[64,512]{1,0:T(8,128)} async-done(((f32[512,512]{1,0:T(8,128)}), f32[64,512]{1,0:T(8,128)}) %reduce-scatter.2.cloned.1.call-update) | async-done | bytes 131088 | tf_op jit(solution)/shard_map/reduce_scatter | solution.py:53
  191.3 1.6 broadcast_multiply_fusion
  (50 shorter events, 7.4 us)
Async XLA Ops:
  7.2 149.8 %copy-start = (bf16[512,64]{0,1:T(8,128)(2,1)S(1)}, bf16[512,64]{0,1:T(8,128)(2,1)}, u32[]{:S(2)}) copy-start(bf16[512,64]{0,1:T(8,128)(2,1)} %param.12) | copy-start | bytes 196612
  7.2 6.8 %copy-start.1 = (f32[16,64,4,128]{3,2,1,0:T(4,128)S(1)}, f32[16,64,4,128]{3,2,1,0:T(4,128)}, u32[]{:S(2)}) copy-start(f32[16,64,4,128]{3,2,1,0:T(4,128)} %param.7) | copy-start | bytes 6291460
  7.2 142.9 %all-gather.2.cloned.1.call-start = ((), (), s32[]{:S(2)}) async-start(), calls=%async_computation.2 | async-start | bytes 5242880 | tf_op jit(solution)/shard_map/all_gather | solution.py:49
  10.2 5.0 %copy-start.4 = (f32[16,64,4,128]{3,0,2,1:T(8,128)}, f32[16,64,4,128]{3,0,2,1:T(8,128)S(1)}, u32[]{:S(2)}) copy-start(f32[16,64,4,128]{3,0,2,1:T(8,128)S(1)} %copy.52) | copy-start | bytes 6291460
  10.2 3.7 %collective-permute-start.1 = (f32[16,1,4,128]{3,0,2,1:T(8,128)S(1)}, f32[16,1,4,128]{3,0,2,1:T(8,128)S(1)}, u32[]{:S(2)}, u32[]{:S(2)}) collective-permute-start(f32[16,1,4,128]{3,0,2,1:T(8,128)S(1)} %get-tuple-element.17), channel_id=1, source_target_pairs={{0,8},{8,16},{16,24},{1,9},{9,17},{17,25},{2,10},{10,18},{18,26},{... | collective-permute-start | bytes 98312 | tf_op jit(solution)/shard_map/ppermute | solution.py:14
  12.6 5.2 %collective-permute-start = (f32[16,1,4,128]{3,0,2,1:T(8,128)S(1)}, f32[16,1,4,128]{3,0,2,1:T(8,128)S(1)}, u32[]{:S(2)}, u32[]{:S(2)}) collective-permute-start(f32[16,1,4,128]{3,0,2,1:T(8,128)S(1)} %get-tuple-element.16), channel_id=1, source_target_pairs={{8,0},{16,8},{24,16},{9,1},{17,9},{25,17},{10,2},{18,10},{26,18},{... | collective-permute-start | bytes 98312 | tf_op jit(solution)/shard_map/ppermute | solution.py:17
  13.9 1.3 copy-start.11
  17.8 15.5 %copy-start.13 = (f32[16,1,4,128]{3,0,2,1:T(8,128)}, f32[16,1,4,128]{3,0,2,1:T(8,128)S(1)}, u32[]{:S(2)}) copy-start(f32[16,1,4,128]{3,0,2,1:T(8,128)S(1)} %collective-permute-done) | copy-start | bytes 98308
  17.8 17.2 %copy-start.2 = (f32[16,66,4,128]{3,0,2,1:T(8,128)}, f32[16,66,4,128]{3,0,2,1:T(8,128)S(1)}, u32[]{:S(2)}) copy-start(f32[16,66,4,128]{3,0,2,1:T(8,128)S(1)} %constant_dynamic-update-slice_fusion) | copy-start | bytes 6488068
  17.9 15.4 %collective-permute-start.2 = (f32[16,66,1,128]{3,0,2,1:T(8,128)S(1)}, f32[16,66,1,128]{3,0,2,1:T(8,128)S(1)}, u32[]{:S(2)}, u32[]{:S(2)}) collective-permute-start(f32[16,66,1,128]{3,0,2,1:T(8,128)S(1)} %get-tuple-element.15), channel_id=1, source_target_pairs={{4,0},{5,1},{6,2},{7,3},{12,8},{13,9},{14,10},{15,11},{20,16},{21,... | collective-permute-start | bytes 1622024 | tf_op jit(solution)/shard_map/ppermute | solution.py:17
  19.2 15.9 %collective-permute-start.3 = (f32[16,66,1,128]{3,0,2,1:T(8,128)S(1)}, f32[16,66,1,128]{3,0,2,1:T(8,128)S(1)}, u32[]{:S(2)}, u32[]{:S(2)}) collective-permute-start(f32[16,66,1,128]{3,0,2,1:T(8,128)S(1)} %get-tuple-element.14), channel_id=1, source_target_pairs={{0,4},{1,5},{2,6},{3,7},{8,12},{9,13},{10,14},{11,15},{16,20},{17,... | collective-permute-start | bytes 1622024 | tf_op jit(solution)/shard_map/ppermute | solution.py:14
  33.3 1.8 copy-start.6
  41.8 10.4 %collective-permute-start.4 = (f32[16,66,6,1]{1,0,3,2:T(8,128)S(1)}, f32[16,66,6,1]{1,0,3,2:T(8,128)S(1)}, u32[]{:S(2)}, u32[]{:S(2)}) collective-permute-start(f32[16,66,6,1]{1,0,3,2:T(8,128)S(1)} %copy.45), channel_id=1, source_target_pairs={{1,0},{2,1},{3,2},{5,4},{6,5},{7,6},{9,8},{10,9},{11,10},{13,12},{... | collective-permute-start | bytes 76040 | tf_op jit(solution)/shard_map/ppermute | solution.py:17
  45.3 9.6 %collective-permute-start.5 = (f32[16,66,6,1]{1,0,3,2:T(8,128)}, f32[16,66,6,1]{1,0,3,2:T(8,128)}, u32[]{:S(2)}, u32[]{:S(2)}) collective-permute-start(f32[16,66,6,1]{1,0,3,2:T(8,128)} %copy.47), channel_id=1, source_target_pairs={{0,1},{1,2},{2,3},{4,5},{5,6},{6,7},{8,9},{9,10},{10,11},{12,13},{... | collective-permute-start | bytes 76040 | tf_op jit(solution)/shard_map/ppermute | solution.py:14
  54.9 3.6 %copy-start.3 = (f32[16,66,4,128]{3,0,2,1:T(8,128)S(1)}, f32[16,66,4,128]{3,0,2,1:T(8,128)}, u32[]{:S(2)}) copy-start(f32[16,66,4,128]{3,0,2,1:T(8,128)} %copy-done.2) | copy-start | bytes 6488068
  54.9 3.6 %copy-start.7 = (f32[16,66,1,128]{3,0,2,1:T(8,128)S(1)}, f32[16,66,1,128]{3,0,2,1:T(8,128)}, u32[]{:S(2)}) copy-start(f32[16,66,1,128]{3,0,2,1:T(8,128)} %copy-done.6) | copy-start | bytes 1622020
  54.9 3.6 %copy-start.9 = (f32[16,66,1,128]{3,0,2,1:T(8,128)S(1)}, f32[16,66,1,128]{3,0,2,1:T(8,128)}, u32[]{:S(2)}) copy-start(f32[16,66,1,128]{3,0,2,1:T(8,128)} %copy-done.8) | copy-start | bytes 1622020
  54.9 3.6 %copy-start.12 = (f32[16,1,4,128]{3,0,2,1:T(8,128)S(1)}, f32[16,1,4,128]{3,0,2,1:T(8,128)}, u32[]{:S(2)}) copy-start(f32[16,1,4,128]{3,0,2,1:T(8,128)} %copy-done.11) | copy-start | bytes 98308
  54.9 3.6 %copy-start.14 = (f32[16,16]{1,0:T(8,128)S(1)}, f32[16,16]{1,0:T(8,128)}, u32[]{:S(2)}) copy-start(f32[16,16]{1,0:T(8,128)} %param.11) | copy-start | bytes 3076
  54.9 3.6 %copy-start.15 = (f32[16]{0:T(128)S(1)}, f32[16]{0:T(128)}, u32[]{:S(2)}) copy-start(f32[16]{0:T(128)} %param.10) | copy-start | bytes 196
  69.1 122.2 %reduce-scatter.2.cloned.1.call-start = ((), (), s32[]{:S(2)}) async-start(), calls=%async_computation.3 | async-start | bytes 1179648 | tf_op jit(solution)/shard_map/reduce_scatter | solution.py:53
  163.9 5.7 %copy-start.5 = (f32[16,64,4,128]{3,0,2,1:T(8,128)S(1)}, f32[16,64,4,128]{3,0,2,1:T(8,128)}, u32[]{:S(2)}) copy-start(f32[16,64,4,128]{3,0,2,1:T(8,128)} %get-tuple-element.22) | copy-start | bytes 6291460
  166.1 13.8 %all-to-all-start = ((bf16[64,4,1024]{2,0,1:T(8,128)(2,1)}), bf16[64,4,1024]{2,0,1:T(8,128)(2,1)S(1)}, u32[]{:S(2)}, u32[]{:S(2)}) async-start(bf16[64,4,1024]{2,0,1:T(8,128)(2,1)} %reshape.22), calls=%async_computation.1 | async-start | bytes 1048576 | tf_op jit(solution)/shard_map/all_to_all | solution.py:66
  169.6 10.6 %copy-start.10 = (f32[256,64]{0,1:T(8,128)S(1)}, f32[256,64]{0,1:T(8,128)}, u32[]{:S(2)}) copy-start(f32[256,64]{0,1:T(8,128)} %param.13) | copy-start | bytes 196612
  (1 other events, 0.8 us)
Sparse Core Ops, SparseCore 0:
  69.3 80.7 all-gather.1
  157.1 34.1 reduce-scatter.1
where the time goes:
time: 200 us
  waiting for transfers between devices  113 us (56%)
  matrix products  25.7 us (13%)
  local copies, waits for them, and re-layouts  25.3 us (13%)
  starting transfers between devices  19.8 us (10%)
  between operations  14.3 us (7%)
    all_gather x1, waiting for transfers between devices, shards(): gathered = lax.all_gather(snapshot, 'ga', axis=3, tiled=True)  80.7 us
    ppermute x3, starting transfers between devices, with_halo(): lax.ppermute(lax.slice_in_dim(block, block.shape[dim] - width, None, axis...  12.2 us
    ppermute x3, waiting for transfers between devices, with_halo(): lax.ppermute(lax.slice_in_dim(block, 0, width, axis=dim), axis, backward)  12.1 us
    dot_general x1, matrix products, shards(): jnp.einsum('vw,wyzx->vyzx', reaction, fields, precision=lax.Precision.HIG...  10.6 us
    reduce_scatter x1, waiting for transfers between devices, shards(): lax.psum_scatter(lax.dot_general(unfolded, unfolded, (((0,), (0,)), ((),...  10.1 us
    all_to_all x1, waiting for transfers between devices, shards(): lax.all_to_all(projected, 'gy', split_axis=1, concat_axis=0, tiled=True)  8.14 us
    unnamed x36, local copies, waits for them, and re-layouts  7.19 us
    dot_general x1, matrix products, shards(): jnp.einsum('vyzx,xr->yzvr', gathered, x_factor, preferred_element_type=jn...  6.91 us
  transfers between devices with their start and end apart: 9, of which 6 were waited for; matrix products, arithmetic and copies ran while one was open for 10% of the time, Pallas kernels for 0%

commit v1 on v0

v1 whole, which is shorter than its diff:
```python
import functools

import jax
import jax.numpy as jnp
from jax import lax
from jax.experimental import pallas as pl
from jax.experimental.pallas import tpu as pltpu
from jax.sharding import PartitionSpec as P

time_step = 0.4
TILE = 32
VMEM = pl.BlockSpec(memory_space=pltpu.VMEM)
SMEM = pl.BlockSpec(memory_space=pltpu.SMEM)
f32, bf16 = jnp.float32, jnp.bfloat16


def shift_pairs(count, step):
    return [(i, i + step) for i in range(count) if 0 <= i + step < count]


def ring_pairs(count, step):
    return [(i, (i + step) % count) for i in range(count)]


def pack_kernel(z_cells, single, flags, f_ref, y_first, y_last, x_first, x_last, *z_refs):
    variables, rows, lanes = f_ref.shape
    y_cells = rows // z_cells
    y_first[...] = f_ref[:, :z_cells, :]
    y_last[...] = f_ref[:, rows - z_cells :, :]
    row = lax.broadcasted_iota(jnp.int32, (8, lanes), 0)
    lane = lax.broadcasted_iota(jnp.int32, (8, lanes), 1)
    pick = jnp.where(
        ((row == 0) & (lane == 0)) | ((row == 1) & (lane == lanes - 1)), 1.0, 0.0
    ).astype(bf16)
    for v in range(variables):
        edges = lax.dot_general(
            pick, f_ref[v].astype(bf16), (((1,), (1,)), ((), ())), preferred_element_type=f32
        )
        x_first[:, v * rows : (v + 1) * rows] = edges[0:1, :]
        x_last[:, v * rows : (v + 1) * rows] = edges[1:2, :]
        if single:
            start = jnp.where(flags[0] == 0, z_cells - 1, 0)
            z_refs[0][v] = f_ref[v, pl.ds(start, y_cells, stride=z_cells), :].astype(bf16)
        else:
            z_refs[0][v] = f_ref[v, pl.ds(0, y_cells, stride=z_cells), :].astype(bf16)
            z_refs[1][v] = f_ref[v, pl.ds(z_cells - 1, y_cells, stride=z_cells), :].astype(bf16)


def stencil_kernel(
    z_cells, parts, flags, diffusion, reaction, f_ref, s_ref, vel_ref, y_lo, y_hi, x_lo, x_hi, z_lo, z_hi,
    new_ref, *rest
):
    snaps, (padded, edge, zface) = rest[:parts], rest[parts:]
    variables, rows, lanes = f_ref.shape
    y_cells = rows // z_cells
    pad = -(-z_cells // 8) * 8
    step = pl.program_id(0)
    tile = new_ref.shape[1]
    has_z_lo, has_z_hi, me, is_buffer = flags[0], flags[1], flags[2], flags[3]

    @pl.when(step == 0)
    def _():
        row = lax.broadcasted_iota(jnp.int32, (8, lanes), 0)
        lane = lax.broadcasted_iota(jnp.int32, (8, lanes), 1)
        put = jnp.where(
            ((row == 0) & (lane == 0)) | ((row == 1) & (lane == lanes - 1)), 1.0, 0.0
        ).astype(bf16)
        side = lax.broadcasted_iota(jnp.int32, (8, rows), 0)
        for v in range(variables):
            padded[v, pad : pad + rows, :] = f_ref[v]
            padded[v, pad - z_cells : pad, :] = y_lo[v]
            padded[v, pad + rows : pad + rows + z_cells, :] = y_hi[v]
            low = jnp.broadcast_to(x_lo[:, v * rows : (v + 1) * rows], (8, rows))
            high = jnp.broadcast_to(x_hi[:, v * rows : (v + 1) * rows], (8, rows))
            both = jnp.where(side == 0, low, jnp.where(side == 1, high, 0.0)).astype(bf16)
            edge[v] = lax.dot_general(both, put, (((0,), (0,)), ((), ())), preferred_element_type=f32)
            zface[v, pl.ds(0, y_cells, stride=z_cells), :] = jnp.where(has_z_lo != 0, z_lo[v].astype(f32), 0.0)
            zface[v, pl.ds(z_cells - 1, y_cells, stride=z_cells), :] = jnp.where(
                has_z_hi != 0, z_hi[v].astype(f32), 0.0
            )

    base = step * tile
    lane = lax.broadcasted_iota(jnp.int32, (tile, lanes), 1)
    z_at = lax.rem(lax.broadcasted_iota(jnp.int32, (tile, lanes), 0), z_cells)
    group = variables // parts
    v_x = vel_ref[0] * 0.5
    v_y = vel_ref[1] * 0.5
    v_z = vel_ref[2] * 0.5
    for part in range(parts):
        target = lax.rem(me + part, parts)
        for j in range(group):
            v = target * group + j
            center = padded[v, pl.ds(base + pad, tile), :]
            y_minus = padded[v, pl.ds(base + pad - z_cells, tile), :]
            y_plus = padded[v, pl.ds(base + pad + z_cells, tile), :]
            face = zface[v, pl.ds(base, tile), :]
            z_minus = jnp.where(z_at == 0, face, padded[v, pl.ds(base + pad - 1, tile), :])
            z_plus = jnp.where(z_at == z_cells - 1, face, padded[v, pl.ds(base + pad + 1, tile), :])
            sides = edge[v, pl.ds(base, tile), :]
            x_minus = jnp.where(lane == 0, sides, pltpu.roll(center, 1, 1))
            x_plus = jnp.where(lane == lanes - 1, sides, pltpu.roll(center, lanes - 1, 1))
            laplace = y_plus + y_minus + z_plus + z_minus + x_plus + x_minus - 6.0 * center
            total = diffusion[v] * laplace - (
                v_x * (x_plus - x_minus) + v_y * (y_plus - y_minus) + v_z * (z_plus - z_minus)
            )
            for w in range(variables):
                total = total + reaction[v, w] * padded[w, pl.ds(base + pad, tile), :]
            value = 0.75 * s_ref[v] + 0.25 * (center + time_step * total)
            value = jnp.where(is_buffer != 0, center, value)
            new_ref[v] = value
            snaps[part][j] = value.astype(bf16)


def gram_kernel(z_cells, parts, flags, xf_ref, *refs):
    pieces, (gram_ref, proj_ref, wide, proj) = refs[:parts], refs[parts:]
    group, rows, lanes = pieces[0].shape
    y_cells = rows // z_cells
    rank = xf_ref.shape[0]
    me = flags[2]
    for part in range(parts):
        source = lax.rem(me - part + parts, parts)
        at = pl.multiple_of(source * lanes, lanes)
        for j in range(group):
            wide[j * rows : (j + 1) * rows, pl.ds(at, lanes)] = pieces[part][j]
    data = wide[...]
    gram = lax.dot_general(data, data, (((0,), (0,)), ((), ())), preferred_element_type=f32)
    gram_ref[...] = gram.astype(bf16)
    proj[...] = lax.dot_general(
        data, xf_ref[...], (((1,), (1,)), ((), ())), preferred_element_type=f32
    )
    for z in range(z_cells):
        cols = [proj[pl.ds(j * rows + z, y_cells, stride=z_cells), :] for j in range(group)]
        proj_ref[z] = jnp.concatenate(cols, axis=1).astype(bf16)


def layer_kernel(y_scale, x_scale, gram_ref, full_ref, yf_ref, out_ref):
    owners, own_rows, width = gram_ref.shape
    total = gram_ref[0].astype(f32)
    for i in range(1, owners):
        total = total + gram_ref[i].astype(f32)
    layers = full_ref.shape[1]
    rank = yf_ref.shape[0]
    if own_rows != rank:
        out_ref[...] = jnp.zeros_like(out_ref)
    out_ref[:own_rows, :width] = (total * x_scale).astype(bf16)
    y_size = yf_ref.shape[1]
    for layer in range(layers):
        m = full_ref[:, layer].reshape(y_size, full_ref.shape[3])
        y_gram = lax.dot_general(m, m, (((1,), (1,)), ((), ())), preferred_element_type=f32) * y_scale
        prod = lax.dot_general(
            yf_ref[...], y_gram, (((1,), (0,)), ((), ())), preferred_element_type=f32,
            precision=lax.Precision.HIGHEST,
        )
        out_ref[:rank, width + layer * y_size : width + (layer + 1) * y_size] = prod.astype(bf16)


def last_kernel(width, parts, *refs):
    pieces, (gram_ref, prod_ref) = refs[:parts], refs[parts:]
    total = pieces[0][...].astype(f32)
    for i in range(1, parts):
        total = total + pieces[i][...].astype(f32)
    gram_ref[...] = total[: gram_ref.shape[0], :width]
    layers, rank, y_size = prod_ref.shape
    for layer in range(layers):
        prod_ref[layer] = total[:rank, width + layer * y_size : width + (layer + 1) * y_size]


def call(kernel, out_shapes, in_specs, scratch=(), name=None, flops=0, moved=0):
    return pl.pallas_call(
        kernel,
        out_shape=out_shapes,
        in_specs=in_specs,
        out_specs=[VMEM] * len(out_shapes),
        scratch_shapes=list(scratch),
        name=name,
        cost_estimate=pl.CostEstimate(flops=flops, bytes_accessed=moved, transcendentals=0),
        compiler_params=pltpu.CompilerParams(vmem_limit_bytes=60 * 1024 * 1024),
    )


def shards(fields, section_start, velocity, diffusivity, reaction, x_factor, y_factor):
    sds = jax.ShapeDtypeStruct
    variables, y_cells, z_cells, lanes = fields.shape
    rows = y_cells * z_cells
    n_y, n_z, n_a = (lax.axis_size(a) for a in ("gy", "gz", "ga"))
    g_z, g_a = lax.axis_index("gz"), lax.axis_index("ga")
    single = n_z == 2
    f = fields.reshape(variables, rows, lanes)
    s = section_start.reshape(variables, rows, lanes)
    vel = velocity.reshape(3, rows, lanes)
    x_size = n_a * lanes
    y_size = n_y * y_cells
    rank = x_factor.shape[1]
    group = variables // n_a

    packed = call(
        functools.partial(pack_kernel, z_cells, single),
        [sds((variables, z_cells, lanes), f32)] * 2
        + [sds((1, variables * rows), f32)] * 2
        + [sds((variables, y_cells, lanes), bf16)] * (1 if single else 2),
        [SMEM, VMEM],
        name="pack",
        moved=f.size * 4,
    )(g_z.reshape(1).astype(jnp.int32), f)
    y_first, y_last, x_first, x_last = packed[:4]
    if single:
        face = lax.ppermute(packed[4], "gz", [(0, 1), (1, 0)])
        z_lo = z_hi = face
    else:
        z_hi = lax.ppermute(packed[4], "gz", shift_pairs(n_z, -1))
        z_lo = lax.ppermute(packed[5], "gz", shift_pairs(n_z, 1))
    x_lo = lax.ppermute(x_last, "ga", shift_pairs(n_a, 1))
    x_hi = lax.ppermute(x_first, "ga", shift_pairs(n_a, -1))
    y_lo = lax.ppermute(y_last, "gy", shift_pairs(n_y, 1))
    y_hi = lax.ppermute(y_first, "gy", shift_pairs(n_y, -1))

    flags = jnp.stack([g_z > 0, g_z < n_z - 1, g_a, g_a == n_a - 1]).astype(jnp.int32)
    pad = -(-z_cells // 8) * 8
    tile = TILE

    def by_rows(lead):
        return pl.BlockSpec((lead, tile, lanes), lambda i: (0, i, 0))

    def whole(*shape):
        return pl.BlockSpec(shape, lambda i: (0,) * len(shape))

    results = pl.pallas_call(
        functools.partial(stencil_kernel, z_cells, n_a),
        grid=(rows // tile,),
        out_shape=[sds((variables, rows, lanes), f32)] + [sds((group, rows, lanes), bf16)] * n_a,
        in_specs=[
            SMEM, SMEM, SMEM,
            whole(variables, rows, lanes),
            by_rows(variables),
            by_rows(3),
            whole(variables, z_cells, lanes),
            whole(variables, z_cells, lanes),
            whole(1, variables * rows),
            whole(1, variables * rows),
            whole(variables, y_cells, lanes),
            whole(variables, y_cells, lanes),
        ],
        out_specs=[by_rows(variables)] + [by_rows(group)] * n_a,
        scratch_shapes=[
            pltpu.VMEM((variables, rows + 2 * pad, lanes), f32),
            pltpu.VMEM((variables, rows, lanes), f32),
            pltpu.VMEM((variables, rows, lanes), f32),
        ],
        name="stencil",
        compiler_params=pltpu.CompilerParams(vmem_limit_bytes=60 * 1024 * 1024),
    )(flags, diffusivity, reaction, f, s, vel, y_lo, y_hi, x_lo, x_hi, z_lo, z_hi)
    new_fields, snaps = results[0], results[1:]

    pieces = [snaps[0]] + [
        lax.ppermute(snaps[k], "ga", ring_pairs(n_a, k)) for k in range(1, n_a)
    ]
    gram, proj = call(
        functools.partial(gram_kernel, z_cells, n_a),
        [sds((x_size, x_size), bf16), sds((z_cells, y_cells, group * rank), bf16)],
        [SMEM] + [VMEM] * (n_a + 1),
        scratch=[pltpu.VMEM((group * rows, x_size), bf16), pltpu.VMEM((group * rows, rank), f32)],
        name="gram",
    )(flags, x_factor.T, *pieces)
    owners = n_y * n_z
    gram = gram.reshape(owners, x_size // owners, x_size)
    full = lax.all_to_all(
        proj.reshape(n_y, z_cells // n_y, y_cells, group * rank), "gy", split_axis=0, concat_axis=0, tiled=True
    )
    gram = lax.all_to_all(gram, ("gy", "gz"), split_axis=0, concat_axis=0, tiled=True)
    layers = z_cells // n_y
    payload = call(
        functools.partial(
            layer_kernel, 1.0 / (variables * rank), 1.0 / (variables * rows * owners)
        ),
        [sds((max(x_size // owners, y_factor.shape[1]), x_size + layers * y_size), bf16)],
        [VMEM] * 3,
        name="layer",
    )(gram, full, y_factor.T)[0]
    payloads = [payload] + [lax.ppermute(payload, "ga", ring_pairs(n_a, k)) for k in range(1, n_a)]
    x_gram, products = call(
        functools.partial(last_kernel, x_size, n_a),
        [sds((x_size // owners, x_size), f32), sds((layers, y_factor.shape[1], y_size), f32)],
        [VMEM] * n_a,
        name="last",
    )(*payloads)
    return (
        new_fields.reshape(fields.shape),
        x_gram,
        jnp.swapaxes(products, 1, 2),
    )


def solution(mesh):
    block = P(None, "gy", "gz", "ga")
    in_specs = (block, block, block, P(), P(), P(), P())
    out_specs = (block, P(("gy", "gz"), None), P(("gz", "gy"), None, None))
    return jax.shard_map(shards, mesh=mesh, in_specs=in_specs, out_specs=out_specs, check_vma=False)
```

time: 200 us -> 99.9 us (0.50)
  waiting for transfers between devices: 113 us -> 29.3 us
  matrix products: 25.7 us -> 0 us
  local copies, waits for them, and re-layouts: 25.3 us -> 2.76 us
  blocking collectives: 0 us -> 21.6 us
  Pallas kernels: 0 us -> 19.8 us
  between operations: 14.3 us -> 0.73 us
  starting transfers between devices: 19.8 us -> 24.5 us
    all_gather x1 -> x0, waiting for transfers between devices: 80.7 us -> none  [shards(): gathered = lax.all_gather(snapshot, 'ga', axis=3, tiled=True)]
    dot_general x5 -> x0, matrix products: 25.7 us -> none  [the longest x1 10.6 us: shards(): jnp.einsum('vw,wyzx->vyzx', reaction, fields, precision=lax.Precision.HIG...]
    all_to_all x0 -> x2, blocking collectives: none -> 21.6 us  [the longest x1 13 us: shards(): lax.all_to_all(gram, ('gy', 'gz'), split_axis=0, concat_axis=0, tiled=True)]
    pallas_call x0 -> x5, Pallas kernels: none -> 19.8 us  [the longest x1 9.85 us: shards(): pl.pallas_call(functools.partial(stencil_kernel, z_cells, n_a), grid=(row...]
    ppermute x6 -> x11, waiting for transfers between devices: 13.8 us -> 29.3 us  [the longest x3 16.6 us: shards(): lax.ppermute(snaps[k], 'ga', ring_pairs(n_a, k))]
    reduce_scatter x1 -> x0, waiting for transfers between devices: 10.1 us -> none  [shards(): lax.psum_scatter(lax.dot_general(unfolded, unfolded, (((0,), (0,)), ((),...]
    ppermute x6 -> x11, starting transfers between devices: 16 us -> 24.5 us  [the longest x3 7.55 us: shards(): lax.ppermute(payload, 'ga', ring_pairs(n_a, k))]
    all_to_all x1 -> x0, waiting for transfers between devices: 8.14 us -> none  [shards(): lax.all_to_all(projected, 'gy', split_axis=1, concat_axis=0, tiled=True)]
  transfers between devices with their start and end apart: 9 -> 11, of which waited for: 6 -> 6; matrix products, arithmetic and copies ran while one was open for 10% -> 1% of each run, Pallas kernels for 0% -> 0%
where the time goes in v1:
time: 99.9 us; the launch traced here: 99.3 us
  waiting for transfers between devices  29.3 us (29%)
  starting transfers between devices  24.5 us (25%)
  blocking collectives  21.6 us (22%)
  Pallas kernels  19.8 us (20%)
  local copies, waits for them, and re-layouts  2.76 us (3%)
    ppermute x3, waiting for transfers between devices, shards(): lax.ppermute(snaps[k], 'ga', ring_pairs(n_a, k))  16.6 us
    all_to_all x1, blocking collectives, shards(): lax.all_to_all(gram, ('gy', 'gz'), split_axis=0, concat_axis=0, tiled=True)  13 us
    pallas_call x1, Pallas kernels, shards(): pl.pallas_call(functools.partial(stencil_kernel, z_cells, n_a), grid=(row...  9.85 us
    ppermute x3, waiting for transfers between devices, shards(): lax.ppermute(payload, 'ga', ring_pairs(n_a, k))  9.57 us
    all_to_all x1, blocking collectives, shards(): lax.all_to_all(proj.reshape(n_y, z_cells // n_y, y_cells, group * rank),...  8.61 us
    ppermute x3, starting transfers between devices, shards(): lax.ppermute(payload, 'ga', ring_pairs(n_a, k))  7.55 us
    ppermute x3, starting transfers between devices, shards(): lax.ppermute(snaps[k], 'ga', ring_pairs(n_a, k))  6.63 us
    ppermute x1, starting transfers between devices, shards(): x_lo = lax.ppermute(x_last, 'ga', shift_pairs(n_a, 1))  3.47 us
  transfers between devices with their start and end apart: 11, of which 6 were waited for; matrix products, arithmetic and copies ran while one was open for 1% of the time, Pallas kernels for 0%

profile of v1, /device:TPU:0, one launch (start us, length us, event | category | flops | bytes accessed | tf_op | source)
XLA Modules:
  0.0 99.3 jit_solution(13563151607407925269)
XLA Ops:
  0.6 2.7 %pack.1 = (f32[16,4,128]{2,1,0:T(4,128)}, f32[16,4,128]{2,1,0:T(4,128)}, f32[1,4096]{1,0:T(1,128)}, f32[1,4096]{1,0:T(1,128)}, bf16[16,64,128]{2,1,0:T(8,128)(2,1)}) custom-call(s32[1]{0:T(128)} %bitcast.7.flags, f32[16,256,128]{2,1,0:T(8,128)} %bitcast.14), custom_call_target="tpu_custom_call" | custom-call | bytes 2097152 | tf_op jit(solution)/shard_map/pack/pallas_call | solution.py:196
  3.3 3.0 %collective-permute-start.4 = (bf16[16,64,128]{2,1,0:T(8,128)(2,1)}, bf16[16,64,128]{2,1,0:T(8,128)(2,1)S(1)}, u32[]{:S(2)}, u32[]{:S(2)}) collective-permute-start(bf16[16,64,128]{2,1,0:T(8,128)(2,1)} %get-tuple-element.21), channel_id=1, source_target_pairs={{0,4},{4,0},{1,5},{5,1},{2,6},{6,2},{3,7},{7,3},{8,12},{12,8},{9,1... | collective-permute-start | bytes 786440 | tf_op jit(solution)/shard_map/ppermute | solution.py:207
  6.3 3.5 %collective-permute-start.2 = (f32[1,4096]{1,0:T(1,128)}, f32[1,4096]{1,0:T(1,128)S(1)}, u32[]{:S(2)}, u32[]{:S(2)}) collective-permute-start(f32[1,4096]{1,0:T(1,128)} %get-tuple-element.19), channel_id=1, source_target_pairs={{0,1},{1,2},{2,3},{4,5},{5,6},{6,7},{8,9},{9,10},{10,11},{12,13},{... | collective-permute-start | bytes 49160 | tf_op jit(solution)/shard_map/ppermute | solution.py:212
  9.8 1.3 %collective-permute-start.3 = (f32[1,4096]{1,0:T(1,128)}, f32[1,4096]{1,0:T(1,128)S(1)}, u32[]{:S(2)}, u32[]{:S(2)}) collective-permute-start(f32[1,4096]{1,0:T(1,128)} %get-tuple-element.20), channel_id=1, source_target_pairs={{1,0},{2,1},{3,2},{5,4},{6,5},{7,6},{9,8},{10,9},{11,10},{13,12},{... | collective-permute-start | bytes 49160 | tf_op jit(solution)/shard_map/ppermute | solution.py:213
  11.1 1.3 %collective-permute-start = (f32[16,4,128]{2,1,0:T(4,128)}, f32[16,4,128]{2,1,0:T(4,128)S(1)}, u32[]{:S(2)}, u32[]{:S(2)}) collective-permute-start(f32[16,4,128]{2,1,0:T(4,128)} %get-tuple-element.17), channel_id=1, source_target_pairs={{0,8},{8,16},{16,24},{1,9},{9,17},{17,25},{2,10},{10,18},{18,26},{... | collective-permute-start | bytes 98312 | tf_op jit(solution)/shard_map/ppermute | solution.py:214
  12.4 1.3 %collective-permute-start.1 = (f32[16,4,128]{2,1,0:T(4,128)}, f32[16,4,128]{2,1,0:T(4,128)S(1)}, u32[]{:S(2)}, u32[]{:S(2)}) collective-permute-start(f32[16,4,128]{2,1,0:T(4,128)} %get-tuple-element.18), channel_id=1, source_target_pairs={{8,0},{16,8},{24,16},{9,1},{17,9},{25,17},{10,2},{18,10},{26,18},{... | collective-permute-start | bytes 98312 | tf_op jit(solution)/shard_map/ppermute | solution.py:215
  14.3 1.3 %collective-permute-done.3.x_hi = f32[1,4096]{1,0:T(1,128)S(1)} collective-permute-done((f32[1,4096]{1,0:T(1,128)}, f32[1,4096]{1,0:T(1,128)S(1)}, u32[]{:S(2)}, u32[]{:S(2)}) %collective-permute-start.3) | collective-permute-done | bytes 16416 | tf_op jit(solution)/shard_map/ppermute | solution.py:213
  15.7 1.8 %collective-permute-done.1.y_hi = f32[16,4,128]{2,1,0:T(4,128)S(1)} collective-permute-done((f32[16,4,128]{2,1,0:T(4,128)}, f32[16,4,128]{2,1,0:T(4,128)S(1)}, u32[]{:S(2)}, u32[]{:S(2)}) %collective-permute-start.1) | collective-permute-done | bytes 32800 | tf_op jit(solution)/shard_map/ppermute | solution.py:215
  18.2 9.9 %stencil.1 = (f32[16,256,128]{2,1,0:T(8,128)}, bf16[4,256,128]{2,1,0:T(8,128)(2,1)}, bf16[4,256,128]{2,1,0:T(8,128)(2,1)}, bf16[4,256,128]{2,1,0:T(8,128)(2,1)}, bf16[4,256,128]{2,1,0:T(8,128)(2,1)}) custom-call(s32[4]{0:T(128)} %pad_add_fusion.flags, f32[16]{0:T(128)} %diffusion.1, f32[16,16]{1,0:T(8,128)} %reaction.1, f32[16,256,128]{2,1,0:T(8,128)} %bitcast.15, ...), custom_call_target="tpu_custom_call" | custom-call | tf_op jit(solution)/shard_map/stencil/pallas_call | solution.py:227
  28.0 2.7 %collective-permute-start.5 = (bf16[4,256,128]{2,1,0:T(8,128)(2,1)}, bf16[4,256,128]{2,1,0:T(8,128)(2,1)S(1)}, u32[]{:S(2)}, u32[]{:S(2)}) collective-permute-start(bf16[4,256,128]{2,1,0:T(8,128)(2,1)} %get-tuple-element.24), channel_id=1, source_target_pairs={{0,1},{1,2},{2,3},{3,0},{4,5},{5,6},{6,7},{7,4},{8,9},{9,10},{10,1... | collective-permute-start | bytes 786440 | tf_op jit(solution)/shard_map/ppermute | solution.py:255
  30.7 2.6 %collective-permute-start.6 = (bf16[4,256,128]{2,1,0:T(8,128)(2,1)}, bf16[4,256,128]{2,1,0:T(8,128)(2,1)S(1)}, u32[]{:S(2)}, u32[]{:S(2)}) collective-permute-start(bf16[4,256,128]{2,1,0:T(8,128)(2,1)} %get-tuple-element.25), channel_id=1, source_target_pairs={{0,2},{1,3},{2,0},{3,1},{4,6},{5,7},{6,4},{7,5},{8,10},{9,11},{10,... | collective-permute-start | bytes 786440 | tf_op jit(solution)/shard_map/ppermute | solution.py:255
  33.3 1.4 %collective-permute-start.7 = (bf16[4,256,128]{2,1,0:T(8,128)(2,1)}, bf16[4,256,128]{2,1,0:T(8,128)(2,1)S(1)}, u32[]{:S(2)}, u32[]{:S(2)}) collective-permute-start(bf16[4,256,128]{2,1,0:T(8,128)(2,1)} %get-tuple-element.26), channel_id=1, source_target_pairs={{0,3},{1,0},{2,1},{3,2},{4,7},{5,4},{6,5},{7,6},{8,11},{9,8},{10,9... | collective-permute-start | bytes 786440 | tf_op jit(solution)/shard_map/ppermute | solution.py:255
  34.7 3.7 %collective-permute-done.5.refs_1_ = bf16[4,256,128]{2,1,0:T(8,128)(2,1)S(1)} collective-permute-done((bf16[4,256,128]{2,1,0:T(8,128)(2,1)}, bf16[4,256,128]{2,1,0:T(8,128)(2,1)S(1)}, u32[]{:S(2)}, u32[]{:S(2)}) %collective-permute-start.5) | collective-permute-done | bytes 262176 | tf_op jit(solution)/shard_map/ppermute | solution.py:255
  38.4 12.9 %collective-permute-done.6.refs_2_ = bf16[4,256,128]{2,1,0:T(8,128)(2,1)S(1)} collective-permute-done((bf16[4,256,128]{2,1,0:T(8,128)(2,1)}, bf16[4,256,128]{2,1,0:T(8,128)(2,1)S(1)}, u32[]{:S(2)}, u32[]{:S(2)}) %collective-permute-start.6) | collective-permute-done | bytes 262176 | tf_op jit(solution)/shard_map/ppermute | solution.py:255
  51.3 0.7 copy-done.2
  52.0 3.2 %gram.1 = (bf16[512,512]{1,0:T(8,128)(2,1)}, bf16[4,64,256]{2,1,0:T(8,128)(2,1)}) custom-call(s32[4]{0:T(128)} %pad_add_fusion.flags, bf16[64,512]{1,0:T(8,128)(2,1)} %bitcast.20, bf16[4,256,128]{2,1,0:T(8,128)(2,1)} %get-tuple-element.23.refs_0_, bf16[4,256,128]{2,1,0:T(8,128)(2,1)} %copy-done.1, bf16[4,256,128]{2,1,0:T(8,128)(2,1)} %copy-done.2, ...), custom_call_target="tpu_custom_call" | custom-call | tf_op jit(solution)/shard_map/gram/pallas_call | solution.py:257
  55.3 8.6 %all_to_all.10.full_ref = bf16[4,1,64,256]{3,2,1,0:T(8,128)(2,1)} all-to-all(bf16[4,1,64,256]{3,2,1,0:T(8,128)(2,1)} %bitcast.19), channel_id=1, replica_groups=mesh['gy'=4,'gz'=2,'ga'=4] {'gy'}, dimensions={0} | all-to-all | bytes 262144 | tf_op jit(solution)/shard_map/all_to_all | solution.py:266
  63.9 13.0 %all_to_all.11.gram_ref = bf16[8,64,512]{2,1,0:T(8,128)(2,1)} all-to-all(bf16[8,64,512]{2,1,0:T(8,128)(2,1)} %bitcast.17), channel_id=1, replica_groups=mesh['gy'=4,'gz'=2,'ga'=4] {'gy','gz'}, dimensions={0} | all-to-all | bytes 1048576 | tf_op jit(solution)/shard_map/all_to_all | solution.py:269
  76.8 2.3 %layer.1.refs_0_ = bf16[64,768]{1,0:T(8,128)(2,1)} custom-call(bf16[8,64,512]{2,1,0:T(8,128)(2,1)} %all_to_all.11.gram_ref, bf16[4,1,64,256]{3,2,1,0:T(8,128)(2,1)} %all_to_all.10.full_ref, f32[64,256]{1,0:T(8,128)} %bitcast.21), custom_call_target="tpu_custom_call" | custom-call | tf_op jit(solution)/shard_map/layer/pallas_call | solution.py:271
  79.1 6.0 %collective-permute-start.10 = (bf16[64,768]{1,0:T(8,128)(2,1)}, bf16[64,768]{1,0:T(8,128)(2,1)S(1)}, u32[]{:S(2)}, u32[]{:S(2)}) collective-permute-start(bf16[64,768]{1,0:T(8,128)(2,1)} %layer.1.refs_0_), channel_id=1, source_target_pairs={{0,3},{1,0},{2,1},{3,2},{4,7},{5,4},{6,5},{7,6},{8,11},{9,8},{10,9... | collective-permute-start | bytes 294920 | tf_op jit(solution)/shard_map/ppermute | solution.py:279
  85.1 1.6 %collective-permute-start.9 = (bf16[64,768]{1,0:T(8,128)(2,1)}, bf16[64,768]{1,0:T(8,128)(2,1)S(1)}, u32[]{:S(2)}, u32[]{:S(2)}) collective-permute-start(bf16[64,768]{1,0:T(8,128)(2,1)} %layer.1.refs_0_), channel_id=1, source_target_pairs={{0,2},{1,3},{2,0},{3,1},{4,6},{5,7},{6,4},{7,5},{8,10},{9,11},{10,... | collective-permute-start | bytes 294920 | tf_op jit(solution)/shard_map/ppermute | solution.py:279
  86.7 2.1 %collective-permute-done.10.refs_3_ = bf16[64,768]{1,0:T(8,128)(2,1)S(1)} collective-permute-done((bf16[64,768]{1,0:T(8,128)(2,1)}, bf16[64,768]{1,0:T(8,128)(2,1)S(1)}, u32[]{:S(2)}, u32[]{:S(2)}) %collective-permute-start.10) | collective-permute-done | bytes 98336 | tf_op jit(solution)/shard_map/ppermute | solution.py:279
  88.7 7.5 %collective-permute-done.9.refs_2_ = bf16[64,768]{1,0:T(8,128)(2,1)S(1)} collective-permute-done((bf16[64,768]{1,0:T(8,128)(2,1)}, bf16[64,768]{1,0:T(8,128)(2,1)S(1)}, u32[]{:S(2)}, u32[]{:S(2)}) %collective-permute-start.9) | collective-permute-done | bytes 98336 | tf_op jit(solution)/shard_map/ppermute | solution.py:279
  97.5 1.7 %last.1 = (f32[64,512]{1,0:T(8,128)}, f32[1,64,256]{2,1,0:T(8,128)}) custom-call(bf16[64,768]{1,0:T(8,128)(2,1)} %layer.1.refs_0_, bf16[64,768]{1,0:T(8,128)(2,1)} %copy-done.6, bf16[64,768]{1,0:T(8,128)(2,1)} %copy-done.5, bf16[64,768]{1,0:T(8,128)(2,1)} %copy-done.4), custom_call_target="tpu_custom_call" | custom-call | tf_op jit(solution)/shard_map/last/pallas_call | solution.py:280
  (28 shorter events, 2.7 us)
Async XLA Ops:
  3.3 14.1 %collective-permute-start.4 = (bf16[16,64,128]{2,1,0:T(8,128)(2,1)}, bf16[16,64,128]{2,1,0:T(8,128)(2,1)S(1)}, u32[]{:S(2)}, u32[]{:S(2)}) collective-permute-start(bf16[16,64,128]{2,1,0:T(8,128)(2,1)} %get-tuple-element.21), channel_id=1, source_target_pairs={{0,4},{4,0},{1,5},{5,1},{2,6},{6,2},{3,7},{7,3},{8,12},{12,8},{9,1... | collective-permute-start | bytes 786440 | tf_op jit(solution)/shard_map/ppermute | solution.py:207
  6.3 8.0 %collective-permute-start.2 = (f32[1,4096]{1,0:T(1,128)}, f32[1,4096]{1,0:T(1,128)S(1)}, u32[]{:S(2)}, u32[]{:S(2)}) collective-permute-start(f32[1,4096]{1,0:T(1,128)} %get-tuple-element.19), channel_id=1, source_target_pairs={{0,1},{1,2},{2,3},{4,5},{5,6},{6,7},{8,9},{9,10},{10,11},{12,13},{... | collective-permute-start | bytes 49160 | tf_op jit(solution)/shard_map/ppermute | solution.py:212
  9.8 5.8 %collective-permute-start.3 = (f32[1,4096]{1,0:T(1,128)}, f32[1,4096]{1,0:T(1,128)S(1)}, u32[]{:S(2)}, u32[]{:S(2)}) collective-permute-start(f32[1,4096]{1,0:T(1,128)} %get-tuple-element.20), channel_id=1, source_target_pairs={{1,0},{2,1},{3,2},{5,4},{6,5},{7,6},{9,8},{10,9},{11,10},{13,12},{... | collective-permute-start | bytes 49160 | tf_op jit(solution)/shard_map/ppermute | solution.py:213
  11.1 4.5 %collective-permute-start = (f32[16,4,128]{2,1,0:T(4,128)}, f32[16,4,128]{2,1,0:T(4,128)S(1)}, u32[]{:S(2)}, u32[]{:S(2)}) collective-permute-start(f32[16,4,128]{2,1,0:T(4,128)} %get-tuple-element.17), channel_id=1, source_target_pairs={{0,8},{8,16},{16,24},{1,9},{9,17},{17,25},{2,10},{10,18},{18,26},{... | collective-permute-start | bytes 98312 | tf_op jit(solution)/shard_map/ppermute | solution.py:214
  12.4 5.0 %collective-permute-start.1 = (f32[16,4,128]{2,1,0:T(4,128)}, f32[16,4,128]{2,1,0:T(4,128)S(1)}, u32[]{:S(2)}, u32[]{:S(2)}) collective-permute-start(f32[16,4,128]{2,1,0:T(4,128)} %get-tuple-element.18), channel_id=1, source_target_pairs={{8,0},{16,8},{24,16},{9,1},{17,9},{25,17},{10,2},{18,10},{26,18},{... | collective-permute-start | bytes 98312 | tf_op jit(solution)/shard_map/ppermute | solution.py:215
  14.3 3.1 %copy-start.9 = (f32[1,4096]{1,0:T(1,128)}, f32[1,4096]{1,0:T(1,128)S(1)}, u32[]{:S(2)}) copy-start(f32[1,4096]{1,0:T(1,128)S(1)} %collective-permute-done.2.x_lo) | copy-start | bytes 49156
  15.6 1.8 %copy-start.10 = (f32[1,4096]{1,0:T(1,128)}, f32[1,4096]{1,0:T(1,128)S(1)}, u32[]{:S(2)}) copy-start(f32[1,4096]{1,0:T(1,128)S(1)} %collective-permute-done.3.x_hi) | copy-start | bytes 49156
  15.7 1.8 %copy-start.7 = (f32[16,4,128]{2,1,0:T(4,128)}, f32[16,4,128]{2,1,0:T(4,128)S(1)}, u32[]{:S(2)}) copy-start(f32[16,4,128]{2,1,0:T(4,128)S(1)} %collective-permute-done.y_lo) | copy-start | bytes 98308
  17.4 0.6 copy-start.8
  17.4 0.7 copy-start
  28.0 10.3 %collective-permute-start.5 = (bf16[4,256,128]{2,1,0:T(8,128)(2,1)}, bf16[4,256,128]{2,1,0:T(8,128)(2,1)S(1)}, u32[]{:S(2)}, u32[]{:S(2)}) collective-permute-start(bf16[4,256,128]{2,1,0:T(8,128)(2,1)} %get-tuple-element.24), channel_id=1, source_target_pairs={{0,1},{1,2},{2,3},{3,0},{4,5},{5,6},{6,7},{7,4},{8,9},{9,10},{10,1... | collective-permute-start | bytes 786440 | tf_op jit(solution)/shard_map/ppermute | solution.py:255
  30.7 20.5 %collective-permute-start.6 = (bf16[4,256,128]{2,1,0:T(8,128)(2,1)}, bf16[4,256,128]{2,1,0:T(8,128)(2,1)S(1)}, u32[]{:S(2)}, u32[]{:S(2)}) collective-permute-start(bf16[4,256,128]{2,1,0:T(8,128)(2,1)} %get-tuple-element.25), channel_id=1, source_target_pairs={{0,2},{1,3},{2,0},{3,1},{4,6},{5,7},{6,4},{7,5},{8,10},{9,11},{10,... | collective-permute-start | bytes 786440 | tf_op jit(solution)/shard_map/ppermute | solution.py:255
  33.3 17.9 %collective-permute-start.7 = (bf16[4,256,128]{2,1,0:T(8,128)(2,1)}, bf16[4,256,128]{2,1,0:T(8,128)(2,1)S(1)}, u32[]{:S(2)}, u32[]{:S(2)}) collective-permute-start(bf16[4,256,128]{2,1,0:T(8,128)(2,1)} %get-tuple-element.26), channel_id=1, source_target_pairs={{0,3},{1,0},{2,1},{3,2},{4,7},{5,4},{6,5},{7,6},{8,11},{9,8},{10,9... | collective-permute-start | bytes 786440 | tf_op jit(solution)/shard_map/ppermute | solution.py:255
  38.4 12.9 %copy-start.1 = (bf16[4,256,128]{2,1,0:T(8,128)(2,1)}, bf16[4,256,128]{2,1,0:T(8,128)(2,1)S(1)}, u32[]{:S(2)}) copy-start(bf16[4,256,128]{2,1,0:T(8,128)(2,1)S(1)} %collective-permute-done.5.refs_1_) | copy-start | bytes 786436
  51.2 0.7 copy-start.2
  51.2 0.8 copy-start.3
  79.1 9.6 %collective-permute-start.10 = (bf16[64,768]{1,0:T(8,128)(2,1)}, bf16[64,768]{1,0:T(8,128)(2,1)S(1)}, u32[]{:S(2)}, u32[]{:S(2)}) collective-permute-start(bf16[64,768]{1,0:T(8,128)(2,1)} %layer.1.refs_0_), channel_id=1, source_target_pairs={{0,3},{1,0},{2,1},{3,2},{4,7},{5,4},{6,5},{7,6},{8,11},{9,8},{10,9... | collective-permute-start | bytes 294920 | tf_op jit(solution)/shard_map/ppermute | solution.py:279
  85.1 11.1 %collective-permute-start.9 = (bf16[64,768]{1,0:T(8,128)(2,1)}, bf16[64,768]{1,0:T(8,128)(2,1)S(1)}, u32[]{:S(2)}, u32[]{:S(2)}) collective-permute-start(bf16[64,768]{1,0:T(8,128)(2,1)} %layer.1.refs_0_), channel_id=1, source_target_pairs={{0,2},{1,3},{2,0},{3,1},{4,6},{5,7},{6,4},{7,5},{8,10},{9,11},{10,... | collective-permute-start | bytes 294920 | tf_op jit(solution)/shard_map/ppermute | solution.py:279
  86.7 9.6 %collective-permute-start.8 = (bf16[64,768]{1,0:T(8,128)(2,1)}, bf16[64,768]{1,0:T(8,128)(2,1)S(1)}, u32[]{:S(2)}, u32[]{:S(2)}) collective-permute-start(bf16[64,768]{1,0:T(8,128)(2,1)} %layer.1.refs_0_), channel_id=1, source_target_pairs={{0,1},{1,2},{2,3},{3,0},{4,5},{5,6},{6,7},{7,4},{8,9},{9,10},{10,1... | collective-permute-start | bytes 294920 | tf_op jit(solution)/shard_map/ppermute | solution.py:279
  88.7 7.5 %copy-start.4 = (bf16[64,768]{1,0:T(8,128)(2,1)}, bf16[64,768]{1,0:T(8,128)(2,1)S(1)}, u32[]{:S(2)}) copy-start(bf16[64,768]{1,0:T(8,128)(2,1)S(1)} %collective-permute-done.10.refs_3_) | copy-start | bytes 294916
  96.2 0.6 copy-start.5
  96.9 0.6 copy-start.6
